TPU v7x, 512 devices: a whole 4x4x16 slice. The times are simulated.
512 devices in a mesh: group: 16 (over y, z_hi), seq: 4 (over z_lo), tensor: 8 (over x, core).
Axes of the slice: x: 4, y: 4, z: 16 (z_hi: 4, z_lo: 4; z = z_hi * 4 + z_lo), core: 2. Of those that a mesh axis runs over, the one named last changes fastest.
Arguments:
- span_tokens: bfloat16 [16, 1024, 2048], P('group', 'seq', 'tensor'), may hold values from -6 to 6
- q_weight: bfloat16 [2048, 2048], P(None, 'tensor'), may hold values from -0.125 to 0.125
- kv_weight: bfloat16 [2048, 512], P(None, 'tensor'), may hold values from -0.125 to 0.125
- out_weight: bfloat16 [2048, 2048], P('tensor'), may hold values from -0.1875 to 0.1875
- kv_pool: bfloat16 [256, 128, 512], P('group', None, 'tensor'), may hold values from -55 to 55, as said below
- cache_lengths: int32 [16], replicated, may hold values from 128 to 8192, as said below
- slot_requests: int32 [16], replicated, may hold values from 0 to 15, as said below
- page_table: int32 [16, 16], replicated, may hold values from 0 to 255, as said below
Outputs:
- attended: bfloat16 [16, 1024, 2048], P('group', 'seq', 'tensor')
Inputs may be any that keep to these rules, and one draw needn't show every extreme that they name: `slot_requests`: A permutation; slot j is processed by group j. `page_table`: no pool page is named twice. The window pages of the requests dealt to one group lie 1 in each group's pool. `cache_lengths`: multiples of 128. `kv_pool`: cached keys and values.
All inputs are finite; a program needn't handle non-finite values.
Results may differ from a plain program's by a relative error of at most 0.015.
Values may be sent and summed in bfloat16 or wider, within the bound.
A program may use at most 64 MiB of HBM per device.

v0:
```python
import jax
import jax.numpy as jnp
from jax import lax
from jax.sharding import PartitionSpec as P

HD = 64
KVH = 4
WINDOW = 2048
PAGE = 128


def shifted(block, axis, distance):
    devices = range(lax.axis_size(axis))
    route = [(i - distance, i) for i in devices if i - distance in devices]
    return lax.ppermute(block, axis, route)


def swapped(value, axis, stride):
    return lax.ppermute(value, axis, [(i, i ^ 1 << stride) for i in range(lax.axis_size(axis))])


def rotate(values, positions):
    half_dim = HD // 2
    frequency = jnp.power(jnp.float32(10000.0), -jnp.arange(half_dim, dtype=jnp.float32) / half_dim)
    angles = positions.astype(jnp.float32)[:, None] * frequency[None, :]
    cosine = jnp.cos(angles)[:, None, :]
    sine_part = jnp.sin(angles)[:, None, :]
    front_half = values[..., :half_dim]
    back_half = values[..., half_dim:]
    return jnp.concatenate(
        [front_half * cosine - back_half * sine_part, back_half * cosine + front_half * sine_part],
        axis=-1,
    )


def attend(block_q, block_k, block_v, base_pos):
    query_count = block_q.shape[0]
    key_count = block_k.shape[0]
    scores = jnp.einsum(
        "tkgd,nkd->kgtn", block_q, block_k, preferred_element_type=jnp.float32
    ) * HD ** (-0.5)
    query_at = jnp.arange(query_count, dtype=jnp.int32)[:, None]
    key_at = jnp.arange(key_count, dtype=jnp.int32)[None, :]
    allowed = (key_at > query_at) & (key_at <= query_at + WINDOW) & (base_pos + key_at >= 0)
    masked = jnp.where(allowed, scores, jnp.float32(-1e30))
    row_top = jnp.max(masked, axis=-1, keepdims=True)
    weights = jnp.where(allowed, jnp.exp(masked - row_top), jnp.float32(0.0))
    row_total = jnp.sum(weights, axis=-1)
    rounded = weights.astype(jnp.bfloat16)
    mixed_rows = jnp.einsum("kgtn,nkd->tkgd", rounded, block_v, preferred_element_type=jnp.float32)
    mixed_rows = mixed_rows / jnp.transpose(row_total, (2, 0, 1))[..., None]
    return mixed_rows.astype(jnp.bfloat16).reshape(query_count, -1)


def shards(
    span_tokens, q_weight, kv_weight, out_weight, kv_pool, cache_lengths, slot_requests, page_table
):
    groups = lax.axis_size("group")
    seq_count = lax.axis_size("seq")
    tensor_count = lax.axis_size("tensor")
    group_id = lax.axis_index("group")
    seq_id = lax.axis_index("seq")
    tensor_id = lax.axis_index("tensor")
    local_reqs, seg_len, feat_local = span_tokens.shape
    head_cols = q_weight.shape[1]
    kv_cols = kv_weight.shape[1]
    local_heads = head_cols // HD
    group_heads = kv_cols // HD
    kv_local = max(1, KVH // tensor_count)
    per_kv = local_heads // kv_local
    holds_keys = tensor_id % 2 == 0
    pool_rows = kv_pool.shape[0]
    capacity = pool_rows // groups
    row_count = local_reqs * seg_len
    my_slots = group_id * local_reqs + jnp.arange(local_reqs, dtype=jnp.int32)
    my_requests = slot_requests[my_slots]
    my_lengths = cache_lengths[my_requests]
    project_piece_rows = lax.all_gather(span_tokens, "tensor", axis=2, tiled=True)
    feat_width = project_piece_rows.shape[2]
    flat_rows = project_piece_rows.reshape(row_count, feat_width)
    query_lin = jnp.dot(flat_rows, q_weight, preferred_element_type=jnp.float32)
    fresh_lin = jnp.dot(flat_rows, kv_weight, preferred_element_type=jnp.float32)
    positions = (
        my_lengths[:, None] + seq_id * seg_len + jnp.arange(seg_len, dtype=jnp.int32)[None, :]
    )
    queries = jax.vmap(rotate)(query_lin.reshape(local_reqs, seg_len, local_heads, HD), positions)
    queries = queries.astype(jnp.bfloat16).reshape(local_reqs, seg_len, kv_local, per_kv, HD)
    fresh_heads = fresh_lin.reshape(local_reqs, seg_len, group_heads, HD)
    rotated = jax.vmap(rotate)(fresh_heads, positions)
    span_kv = (
        jnp.where(holds_keys, rotated, fresh_heads)
        .astype(jnp.bfloat16)
        .reshape(local_reqs, seg_len, kv_cols)
    )
    all_ids = page_table[slot_requests]
    owned_here = all_ids // pool_rows == group_id
    slot_rank = jnp.cumsum(owned_here.astype(jnp.int32), axis=1) - 1
    local_rows = all_ids - group_id * pool_rows
    chosen = owned_here[:, :, None] & (
        slot_rank[:, :, None] == jnp.arange(capacity, dtype=jnp.int32)[None, None, :]
    )
    wanted = jnp.sum(jnp.where(chosen, local_rows[:, :, None], 0), axis=1)
    my_ids = page_table[my_requests].reshape(-1)
    my_owner = my_ids // pool_rows
    onehot = (my_owner[:, None] == jnp.arange(groups, dtype=jnp.int32)[None, :]).astype(jnp.int32)
    arrival = jnp.sum((jnp.cumsum(onehot, axis=0) - 1) * onehot, axis=1)
    arrived_row = my_owner * capacity + arrival
    outgoing = kv_pool[wanted]
    arrived = lax.all_to_all(outgoing, "group", split_axis=0, concat_axis=0, tiled=True)
    cached = arrived.reshape(groups * capacity, PAGE, kv_cols)[arrived_row]
    cached = cached.reshape(local_reqs, WINDOW, kv_cols)
    span_all = jnp.zeros((local_reqs, seg_len * seq_count, kv_cols), jnp.bfloat16)
    for back_step in range(seq_count - 1, -1, -1):
        piece_rows = span_kv if back_step == 0 else shifted(span_kv, "seq", back_step)
        span_all = lax.dynamic_update_slice_in_dim(
            span_all, piece_rows, (seq_id - back_step) * seg_len, 1
        )
    joined = jnp.concatenate([cached, span_all], axis=1)
    visible = lax.dynamic_slice_in_dim(joined, seq_id * seg_len, WINDOW + seg_len, 1)
    partner_rows = swapped(visible, "tensor", 0)
    key_all = jnp.where(holds_keys, visible, partner_rows).reshape(
        local_reqs, WINDOW + seg_len, group_heads, HD
    )
    value_all = jnp.where(holds_keys, partner_rows, visible).reshape(
        local_reqs, WINDOW + seg_len, group_heads, HD
    )
    block_len = min(128, seg_len)
    block_count = seg_len // block_len

    def per_request(request_items):
        request_q, request_k, request_v, length = request_items

        def per_block(block_index):
            first_row = block_index * block_len
            block_q = lax.dynamic_slice_in_dim(request_q, first_row, block_len, 0)
            block_k = lax.dynamic_slice_in_dim(request_k, first_row, WINDOW + block_len, 0)
            block_v = lax.dynamic_slice_in_dim(request_v, first_row, WINDOW + block_len, 0)
            return attend(block_q, block_k, block_v, length - WINDOW + seq_id * seg_len + first_row)

        return lax.map(per_block, jnp.arange(block_count, dtype=jnp.int32)).reshape(
            seg_len, head_cols
        )

    attended_heads = lax.map(per_request, (queries, key_all, value_all, my_lengths))
    flat_heads = attended_heads.reshape(row_count, head_cols)
    out_cols = out_weight.shape[1] // tensor_count
    summed = lax.psum_scatter(
        lax.dot_general(
            out_weight, flat_heads, (((0,), (1,)), ((), ())), preferred_element_type=jnp.float32
        ).astype(jnp.bfloat16),
        "tensor",
        scatter_dimension=0,
        tiled=True,
    ).astype(jnp.float32)
    result = summed.T
    return result.astype(jnp.bfloat16).reshape(local_reqs, seg_len, out_cols)


def solution(mesh):
    placed = (
        P("group", "seq", "tensor"),
        P(None, "tensor"),
        P(None, "tensor"),
        P("tensor", None),
        P("group", None, "tensor"),
        P(),
        P(),
        P(),
    )
    return jax.shard_map(
        shards, mesh=mesh, in_specs=placed, out_specs=P("group", "seq", "tensor"), check_vma=False
    )
```

profile of v0, /device:TPU:24, one launch (start us, length us, event | category | flops | bytes accessed | tf_op | source)
XLA Modules:
  0.0 120.5 jit_solution(13842631607931138313)
XLA Ops:
  6.5 0.0 copy-start
  6.5 0.0 copy-start.1
  6.5 0.0 all-gather.2.cloned.1.call-start
  6.5 0.7 all-gather.2.cloned.1.call-update
  7.3 1.3 %dynamic-slice.10 = s32[1]{0:T(128)} dynamic-slice(s32[16]{0:T(128)} %param.16, s32[]{:T(128)} %bitcast.20), dynamic_slice_sizes={1} | dynamic-slice | bytes 12 | tf_op jit(solution)/shard_map/gather | solution.py:76
  10.5 0.7 compare_select_fusion.2
  11.2 1.3 %gather_fusion = s32[16,16]{1,0:T(8,128)S(1)} fusion(s32[16,16]{1,0:T(8,128)} %param.17, s32[1024]{0:T(1024)S(1)} %pad_clamp_fusion.2), kind=kCustom, calls=%fused_computation | custom fusion | bytes 2112 | tf_op jit(solution)/shard_map/gather | solution.py:95
  12.5 0.2 reduce_window_sum.22
  12.7 0.1 select_reduce_fusion.1
  12.8 2.2 %gather_fusion.1 = bf16[16,128,64]{1,2,0:T(8,128)(2,1)} fusion(bf16[16,128,64]{1,2,0:T(8,128)(2,1)} %param.14, s32[1024]{0:T(1024)S(1)} %pad_clamp_fusion.1), kind=kCustom, calls=%fused_computation.1 | custom fusion | bytes 524352 | tf_op jit(solution)/shard_map/gather | solution.py:108
  15.0 18.0 %all-to-all-start = ((bf16[16,1,128,64]{2,3,1,0:T(8,128)(2,1)}), bf16[16,1,128,64]{2,3,1,0:T(8,128)(2,1)S(1)}, u32[]{:S(2)}, u32[]{:S(2)}) async-start(bf16[16,1,128,64]{2,3,1,0:T(8,128)(2,1)} %bitcast.17), calls=%async_computation | async-start | bytes 524288 | tf_op jit(solution)/shard_map/all_to_all | solution.py:109
  33.0 0.0 reduce-scatter.2.cloned.1.call-start
  33.1 0.1 fusion.47
  33.1 1.2 %dynamic-slice.12 = s32[1]{0:T(128)} dynamic-slice(s32[16]{0:T(128)} %param.15, s32[]{:T(128)} %bitcast.21), dynamic_slice_sizes={1} | dynamic-slice | bytes 12 | tf_op jit(solution)/shard_map/gather | solution.py:77
  34.4 1.5 %copy.21 = bf16[2048,256]{0,1:T(8,128)(2,1)S(1)} copy(bf16[2048,256]{1,0:T(8,128)(2,1)} %param.11) | data formatting | bytes 2097152 | tf_op args[1]
  37.1 0.2 select_reduce_fusion
  37.3 0.7 fusion.51
  38.0 0.2 multiply_cosine_fusion
  38.2 12.8 %all-to-all-done = bf16[16,1,128,64]{2,3,1,0:T(8,128)(2,1)S(1)} async-done(((bf16[16,1,128,64]{2,3,1,0:T(8,128)(2,1)}), bf16[16,1,128,64]{2,3,1,0:T(8,128)(2,1)S(1)}, u32[]{:S(2)}, u32[]{:S(2)}) %all-to-all-start) | async-done | bytes 262176 | tf_op jit(solution)/shard_map/all_to_all | solution.py:109
  51.0 0.6 gather_fusion.2
  51.6 0.2 copy.20
  51.8 0.1 reshape.403
  51.9 0.0 all-gather.2.cloned.1.call-done
  51.9 0.0 copy-done.1
  52.0 1.7 %fusion.30 = f32[256,64]{0,1:T(8,128)S(1)} fusion(bf16[2048,64]{0,1:T(8,128)(2,1)S(1)} %copy-done.1, bf16[1,256,2048]{2,1,0:T(8,128)(2,1)} %all-gather.2.cloned.1.call-done), kind=kOutput, calls=%fused_computation.35 | convolution fusion | flops 67108864 | bytes 1376256 | tf_op jit(solution)/shard_map/dot_general | solution.py:82
  53.6 0.2 fusion.41
  53.8 3.8 %collective-permute-start = (bf16[1,256,64]{1,2,0:T(8,128)(2,1)S(1)}, bf16[1,256,64]{1,2,0:T(8,128)(2,1)S(1)}, u32[]{:S(2)}, u32[]{:S(2)}) collective-permute-start(bf16[1,256,64]{1,2,0:T(8,128)(2,1)S(1)} %fusion.44), channel_id=1, source_target_pairs={{0,24},{1,25},{2,26},{3,27},{4,28},{5,29},{6,30},{7,31},{32,56},{3... | collective-permute-start | bytes 98312 | tf_op jit(solution)/shard_map/ppermute | solution.py:15
  57.6 3.6 %collective-permute-start.1 = (bf16[1,256,64]{1,2,0:T(8,128)(2,1)S(1)}, bf16[1,256,64]{1,2,0:T(8,128)(2,1)S(1)}, u32[]{:S(2)}, u32[]{:S(2)}) collective-permute-start(bf16[1,256,64]{1,2,0:T(8,128)(2,1)S(1)} %fusion.44), channel_id=1, source_target_pairs={{0,16},{8,24},{1,17},{9,25},{2,18},{10,26},{3,19},{11,27},{4,20},{... | collective-permute-start | bytes 98312 | tf_op jit(solution)/shard_map/ppermute | solution.py:15
  61.2 1.3 %collective-permute-start.2 = (bf16[1,256,64]{1,2,0:T(8,128)(2,1)S(1)}, bf16[1,256,64]{1,2,0:T(8,128)(2,1)S(1)}, u32[]{:S(2)}, u32[]{:S(2)}) collective-permute-start(bf16[1,256,64]{1,2,0:T(8,128)(2,1)S(1)} %fusion.44), channel_id=1, source_target_pairs={{0,8},{8,16},{16,24},{1,9},{9,17},{17,25},{2,10},{10,18},{18,26},{... | collective-permute-start | bytes 98312 | tf_op jit(solution)/shard_map/ppermute | solution.py:15
  62.5 1.7 %convolution_bitcast_fusion = f32[1,256,4,64]{1,3,2,0:T(8,128)S(1)} fusion(bf16[4,64,2048]{2,1,0:T(8,128)(2,1)S(1)} %bitcast.138, bf16[1,256,2048]{2,1,0:T(8,128)(2,1)} %all-gather.2.cloned.1.call-done), kind=kOutput, calls=%fused_computation.33 | convolution fusion | flops 268435456 | bytes 2359296 | tf_op jit(solution)/shard_map/dot_general | solution.py:81
  64.2 0.0 collective-permute-done
  64.3 0.0 collective-permute-done.1
  64.3 0.0 collective-permute-done.2
  64.4 0.1 fusion.32
  64.5 1.9 %collective-permute-start.3 = (bf16[1,2304,64]{1,2,0:T(8,128)(2,1)S(1)}, bf16[1,2304,64]{1,2,0:T(8,128)(2,1)S(1)}, u32[]{:S(2)}, u32[]{:S(2)}) collective-permute-start(bf16[1,2304,64]{1,2,0:T(8,128)(2,1)S(1)} %fusion.32), channel_id=1, source_target_pairs={{0,1},{1,0},{2,3},{3,2},{4,5},{5,4},{6,7},{7,6},{8,9},{9,8},{10,11... | collective-permute-start | bytes 884744 | tf_op jit(solution)/shard_map/ppermute | solution.py:19
  66.5 1.5 %collective-permute-done.3 = bf16[1,2304,64]{1,2,0:T(8,128)(2,1)S(1)} collective-permute-done((bf16[1,2304,64]{1,2,0:T(8,128)(2,1)S(1)}, bf16[1,2304,64]{1,2,0:T(8,128)(2,1)S(1)}, u32[]{:S(2)}, u32[]{:S(2)}) %collective-permute-start.3) | collective-permute-done | bytes 294944 | tf_op jit(solution)/shard_map/ppermute | solution.py:19
  68.0 9.9 %while.22 = (s32[]{:T(128)}, bf16[2,128,256]{2,1,0:T(8,128)(2,1)S(1)}, s32[2]{0:T(128)S(1)}, bf16[2304,1,64]{0,2,1:T(8,128)(2,1)S(1)}, s32[]{:T(128)}, /*index=5...) while((s32[]{:T(128)}, ...), condition=%wide.region_7.8_spmd, body=%wide.region_4.7_spmd.sunk | while | flops 296422784 | bytes 15449576 | solution.py:140
  68.0 0.6 dynamic_slice.67
  69.2 1.2 fusion.66
  70.4 0.8 fusion.67
  71.2 0.8 fusion.68
  72.0 0.8 fusion.69
  72.8 0.1 copy.27
  73.0 0.6 dynamic_slice.67
  74.2 1.2 fusion.66
  75.4 0.8 fusion.67
  76.1 0.8 fusion.68
  77.0 0.8 fusion.69
  77.8 0.1 copy.27
  77.9 0.0 copy-done
  77.9 1.4 %fusion.28 = bf16[2048,256]{0,1:T(8,128)(2,1)} fusion(bf16[256,256]{1,0:T(8,128)(2,1)S(1)} %bitcast.140, bf16[256,2048]{1,0:T(8,128)(2,1)S(1)} %copy-done), kind=kOutput, calls=%fused_computation.32 | convolution fusion | flops 268959744 | bytes 2228224 | tf_op jit(solution)/shard_map/dot_general | solution.py:148
  79.4 0.0 reduce-scatter.2.cloned.1.call-update
  79.4 34.3 %reduce-scatter.2.cloned.1.call-done = bf16[256,256]{0,1:T(8,128)(2,1)} async-done(((bf16[2048,256]{0,1:T(8,128)(2,1)}), bf16[256,256]{0,1:T(8,128)(2,1)}) %reduce-scatter.2.cloned.1.call-update) | async-done | bytes 131088 | tf_op jit(solution)/shard_map/reduce_scatter | solution.py:147
  (25 shorter events, 0.3 us)
Async XLA Ops:
  6.5 71.4 %copy-start = (bf16[256,2048]{1,0:T(8,128)(2,1)S(1)}, bf16[256,2048]{1,0:T(8,128)(2,1)}, u32[]{:S(2)}) copy-start(bf16[256,2048]{1,0:T(8,128)(2,1)} %param.13) | copy-start | bytes 3145732
  6.5 45.4 %copy-start.1 = (bf16[2048,64]{0,1:T(8,128)(2,1)S(1)}, bf16[2048,64]{0,1:T(8,128)(2,1)}, u32[]{:S(2)}) copy-start(bf16[2048,64]{0,1:T(8,128)(2,1)} %param.12) | copy-start | bytes 786436
  6.5 45.4 %all-gather.2.cloned.1.call-start = ((), (), s32[]{:S(2)}) async-start(), calls=%async_computation.2 | async-start | bytes 1179648 | tf_op jit(solution)/shard_map/all_gather | solution.py:78
  15.0 36.0 %all-to-all-start = ((bf16[16,1,128,64]{2,3,1,0:T(8,128)(2,1)}), bf16[16,1,128,64]{2,3,1,0:T(8,128)(2,1)S(1)}, u32[]{:S(2)}, u32[]{:S(2)}) async-start(bf16[16,1,128,64]{2,3,1,0:T(8,128)(2,1)} %bitcast.17), calls=%async_computation | async-start | bytes 524288 | tf_op jit(solution)/shard_map/all_to_all | solution.py:109
  33.0 80.7 %reduce-scatter.2.cloned.1.call-start = ((), (), s32[]{:S(2)}) async-start(), calls=%async_computation.3 | async-start | bytes 1179648 | tf_op jit(solution)/shard_map/reduce_scatter | solution.py:147
  53.8 10.4 %collective-permute-start = (bf16[1,256,64]{1,2,0:T(8,128)(2,1)S(1)}, bf16[1,256,64]{1,2,0:T(8,128)(2,1)S(1)}, u32[]{:S(2)}, u32[]{:S(2)}) collective-permute-start(bf16[1,256,64]{1,2,0:T(8,128)(2,1)S(1)} %fusion.44), channel_id=1, source_target_pairs={{0,24},{1,25},{2,26},{3,27},{4,28},{5,29},{6,30},{7,31},{32,56},{3... | collective-permute-start | bytes 98312 | tf_op jit(solution)/shard_map/ppermute | solution.py:15
  57.6 6.6 %collective-permute-start.1 = (bf16[1,256,64]{1,2,0:T(8,128)(2,1)S(1)}, bf16[1,256,64]{1,2,0:T(8,128)(2,1)S(1)}, u32[]{:S(2)}, u32[]{:S(2)}) collective-permute-start(bf16[1,256,64]{1,2,0:T(8,128)(2,1)S(1)} %fusion.44), channel_id=1, source_target_pairs={{0,16},{8,24},{1,17},{9,25},{2,18},{10,26},{3,19},{11,27},{4,20},{... | collective-permute-start | bytes 98312 | tf_op jit(solution)/shard_map/ppermute | solution.py:15
  61.2 3.1 %collective-permute-start.2 = (bf16[1,256,64]{1,2,0:T(8,128)(2,1)S(1)}, bf16[1,256,64]{1,2,0:T(8,128)(2,1)S(1)}, u32[]{:S(2)}, u32[]{:S(2)}) collective-permute-start(bf16[1,256,64]{1,2,0:T(8,128)(2,1)S(1)} %fusion.44), channel_id=1, source_target_pairs={{0,8},{8,16},{16,24},{1,9},{9,17},{17,25},{2,10},{10,18},{18,26},{... | collective-permute-start | bytes 98312 | tf_op jit(solution)/shard_map/ppermute | solution.py:15
  64.5 3.5 %collective-permute-start.3 = (bf16[1,2304,64]{1,2,0:T(8,128)(2,1)S(1)}, bf16[1,2304,64]{1,2,0:T(8,128)(2,1)S(1)}, u32[]{:S(2)}, u32[]{:S(2)}) collective-permute-start(bf16[1,2304,64]{1,2,0:T(8,128)(2,1)S(1)} %fusion.32), channel_id=1, source_target_pairs={{0,1},{1,0},{2,3},{3,2},{4,5},{5,4},{6,7},{7,6},{8,9},{9,8},{10,11... | collective-permute-start | bytes 884744 | tf_op jit(solution)/shard_map/ppermute | solution.py:19
Sparse Core Ops, SparseCore 0:
  9.4 35.1 all-gather.1
  79.5 34.1 reduce-scatter.1
where the time goes:
time: 121 us
  waiting for transfers between devices  49.4 us (41%)
  starting transfers between devices  28.6 us (24%)
  between operations  16.8 us (14%)
  local copies, waits for them, and re-layouts  9.88 us (8%)
  matrix products  7.99 us (7%)
  other arithmetic  6.69 us (6%)
  loops' own time  1.28 us (1%)
    reduce_scatter x1, waiting for transfers between devices, shards(): lax.psum_scatter(lax.dot_general(out_weight, flat_heads, (((0,), (1,)), (...  34.3 us
    all_to_all x1, starting transfers between devices, shards(): lax.all_to_all(outgoing, 'group', split_axis=0, concat_axis=0, tiled=True)  18 us
    all_to_all x1, waiting for transfers between devices, shards(): lax.all_to_all(outgoing, 'group', split_axis=0, concat_axis=0, tiled=True)  12.8 us
    ppermute x3, starting transfers between devices, shifted(): return lax.ppermute(block, axis, route)  8.66 us
  transfers between devices with their start and end apart: 7, of which 3 were waited for; matrix products, arithmetic and copies ran while one was open for 10% of the time, Pallas kernels for 0%

commit v1 on v0

v1 whole, which is shorter than its diff:
```python
import functools

import jax
import jax.numpy as jnp
from jax import lax
from jax.experimental import pallas as pl
from jax.experimental.pallas import tpu as pltpu
from jax.sharding import PartitionSpec as P

HD = 64
WINDOW = 2048
PAGE = 128
MESH = pl.DeviceIdType.MESH
NEG = -1e30
FLOOR = -1e20
F32 = jnp.float32
BF16 = jnp.bfloat16


def layer_kernel(
    wanted_ref, place_ref, length_ref, cos_ref, sin_ref, x_ref, qw_ref, kvw_ref, ow_ref, pool_ref,
    out_ref,
    xs, outp, kv, fresh, qacc, kvacc, qt, acc, top, tot, thr_ref, part, mine, pairin, bsum, landed, relay,
    x_send, x_recv, xf_send, xf_recv, p_send, p_recv, pf_send, pf_recv,
    n_send, n_recv, nf_send, nf_recv, r_send, r_recv, s_send, s_recv,
):
    group = lax.axis_index("group")
    seq = lax.axis_index("seq")
    tensor = lax.axis_index("tensor")
    chip = tensor // 2
    core = tensor % 2
    gy = group // 4
    gz = group % 4
    partner = {"tensor": chip * 2 + (1 - core)}

    def chip_at(d):
        return {"tensor": ((chip + d) % 4) * 2 + core}

    def group_to(s):
        dy, dz = s // 4, s % 4
        return ((gy + dy) % 4) * 4 + (gz + dz) % 4

    def group_from(s):
        dy, dz = s // 4, s % 4
        return ((gy - dy + 4) % 4) * 4 + (gz - dz + 4) % 4

    def page_dev(s):
        if s % 4 == 2:
            return {"group": group_to(s), "seq": seq + 1 - 2 * (seq % 2)}
        return {"group": group_to(s)}

    def remote(src, dst, ss, rs, dev):
        return pltpu.make_async_remote_copy(
            src_ref=src, dst_ref=dst, send_sem=ss, recv_sem=rs, device_id=dev, device_id_type=MESH
        )

    barrier = pltpu.get_barrier_semaphore()
    for s in range(1, 16):
        pl.semaphore_signal(barrier, inc=1, device_id=page_dev(s), device_id_type=MESH)
    for b in range(1, 4):
        pl.semaphore_signal(barrier, inc=1, device_id={"seq": (seq + b) % 4}, device_id_type=MESH)
    for d in range(1, 4):
        if d != 2:
            pl.semaphore_signal(barrier, inc=1, device_id=chip_at(d), device_id_type=MESH)
    pl.semaphore_signal(barrier, inc=1, device_id=partner, device_id_type=MESH)

    for s in range(1, 16):
        outp[s - 1] = pool_ref[wanted_ref[group_to(s)]]
    kv[core, 0] = pool_ref[wanted_ref[group]]
    thr_ref[...] = jnp.maximum(
        lax.broadcasted_iota(jnp.int32, (1, 256), 1) + seq * 256, WINDOW - 1 - length_ref[0]
    )
    for h in range(4):
        acc[h] = jnp.zeros((HD, 256), F32)
        top[h] = jnp.full((1, 256), FLOOR, F32)
        tot[h] = jnp.zeros((1, 256), F32)

    pl.semaphore_wait(barrier, 21)

    first = {d: remote(x_ref, xs.at[0, 4 - d], x_send.at[d], x_recv.at[4 - d], chip_at(d)) for d in (1, 3)}
    own_x = remote(x_ref, xs.at[1, 0], xf_send.at[0], xf_recv.at[0], partner)
    for d in (1, 3):
        first[d].start()
    own_x.start()
    order = [1, 3, 4, 8, 12, 5, 7, 9, 11, 13, 15, 2, 6, 10, 14]
    pages = {
        s: remote(outp.at[s - 1], kv.at[core, s], p_send.at[s], p_recv.at[s], page_dev(s)) for s in order
    }
    for s in (2, 6, 10, 14, 1, 3, 5, 7, 9, 11, 13, 15, 4, 8, 12):
        pages[s].start()
    pagef = {
        s: remote(kv.at[core, s], kv.at[core, s], pf_send.at[s], pf_recv.at[s], partner) for s in range(16)
    }
    pagef[0].start()

    def project(p, d):
        block = x_ref[...] if (p, d) == (0, 0) else xs[p, d]
        t = ((chip + d) % 4) * 2 + (core if p == 0 else 1 - core)
        rows = pl.ds(pl.multiple_of(t * 256, 256), 256)
        q = jnp.dot(block, qw_ref[rows, :], preferred_element_type=F32)
        f = lax.dot_general(kvw_ref[:, rows], block, (((1,), (1,)), ((), ())), preferred_element_type=F32)
        if (p, d) == (0, 0):
            qacc[...] = q
            kvacc[...] = f
        else:
            qacc[...] += q
            kvacc[...] += f

    project(0, 0)
    xf = {d: remote(xs.at[0, d], xs.at[1, d], xf_send.at[d], xf_recv.at[d], partner) for d in (1, 2, 3)}
    from_slot = 3 - 2 * core
    on = {"tensor": ((chip + 1 + 2 * core) % 4) * 2 + core}
    first[3].wait_recv()
    first[1].wait_recv()
    second = remote(xs.at[0, from_slot], xs.at[0, 2], x_send.at[2], x_recv.at[2], on)
    second.start()
    xf[1].start()
    xf[3].start()
    own_x.wait_recv()
    project(1, 0)
    project(0, 1)
    project(0, 3)
    xf[1].wait_recv()
    project(1, 1)
    xf[3].wait_recv()
    project(1, 3)
    second.wait_recv()
    xf[2].start()
    project(0, 2)
    xf[2].wait_recv()
    project(1, 2)

    is_key = jnp.where(core == 0, 1.0, 0.0).astype(F32)
    cos = cos_ref[...]
    sin = sin_ref[...]
    kcos = cos * is_key + (1.0 - is_key)
    ksin = sin * is_key
    a = kvacc[:32, :]
    b = kvacc[32:, :]
    fresh[core, 0] = jnp.concatenate([a * kcos - b * ksin, b * kcos + a * ksin], axis=0).astype(BF16)
    for step in range(1, 4):
        @pl.when(seq + step < 4)
        def _():
            remote(
                fresh.at[core, 0], fresh.at[core, step], n_send.at[step], n_recv.at[step], {"seq": (seq + step) % 4}
            ).start()
    newf = {
        i: remote(fresh.at[core, i], fresh.at[core, i], nf_send.at[i], nf_recv.at[i], partner) for i in range(4)
    }
    newf[0].start()
    for h in range(4):
        w = qacc[:, h * HD:(h + 1) * HD].T
        a = w[:32, :] * 0.125
        b = w[32:, :] * 0.125
        qt[h] = jnp.concatenate([a * cos - b * sin, b * cos + a * sin], axis=0).astype(BF16)

    def fold(keys, values, mask):
        kb = keys.T

        def head(h, carry):
            s = jnp.dot(kb, qt[h], preferred_element_type=F32)
            s = mask(s)
            old = top[h]
            new = jnp.maximum(old, jnp.max(s, axis=0, keepdims=True))
            p = jnp.exp(s - new)
            alpha = jnp.exp(old - new)
            top[h] = new
            tot[h] = tot[h] * alpha + jnp.sum(p, axis=0, keepdims=True)
            acc[h] = acc[h] * alpha + jnp.dot(values, p.astype(BF16), preferred_element_type=F32)
            return carry

        lax.fori_loop(0, 4, head, 0)

    row = lax.broadcasted_iota(jnp.int32, (PAGE, 256), 0)

    def fold_pages(slots):
        def mask(s):
            pieces = []
            for i, slot in enumerate(slots):
                low = thr_ref[...] - place_ref[group_from(slot)] * PAGE
                pieces.append(jnp.where(row > low, s[i * PAGE:(i + 1) * PAGE], NEG))
            return jnp.concatenate(pieces, axis=0)

        fold(
            jnp.concatenate([kv[0, s] for s in slots], axis=1),
            jnp.concatenate([kv[1, s] for s in slots], axis=1),
            mask,
        )

    def take(slots):
        for s in slots:
            pages[s].wait_recv()
            pagef[s].start()

    def ready(slots):
        for s in slots:
            remote(kv.at[core, s], kv.at[1 - core, s], pf_send.at[s], pf_recv.at[s], partner).wait_recv()

    causal = lax.broadcasted_iota(jnp.int32, (256, 256), 0) <= lax.broadcasted_iota(jnp.int32, (256, 256), 1)

    def new_ready(i):
        remote(fresh.at[core, i], fresh.at[1 - core, i], nf_send.at[i], nf_recv.at[i], partner).wait_recv()

    new_ready(0)
    fold(fresh[0, 0], fresh[1, 0], lambda s: jnp.where(causal, s, NEG))
    c0, c1, c2, c3 = [0, 4, 8, 12], [1, 3, 5, 7], [9, 11, 13, 15], [2, 6, 10, 14]
    take(c0[1:])
    take(c1)
    ready(c0)
    fold_pages(c0)
    take(c2)
    ready(c1)
    fold_pages(c1)
    take(c3)
    ready(c2)
    fold_pages(c2)
    for step in range(1, 4):
        @pl.when(seq >= step)
        def _():
            remote(
                fresh.at[core, 0], fresh.at[core, step], n_send.at[step], n_recv.at[step], {"seq": (seq + step) % 4}
            ).wait_recv()
            newf[step].start()
    ready(c3)
    fold_pages(c3)
    for step in range(1, 4):
        @pl.when(seq >= step)
        def _():
            new_ready(step)
            fold(fresh[0, step], fresh[1, step], lambda s: s)

    heads = jnp.concatenate([(acc[h] / tot[h]).T.astype(BF16) for h in range(4)], axis=1)

    def partial_for(d, c):
        cols = pl.ds(pl.multiple_of((((chip + d) % 4) * 2 + c) * 256, 256), 256)
        return jnp.dot(heads, ow_ref[:, cols], preferred_element_type=F32).astype(BF16)

    near = 1 + 2 * core
    far = 3 - 2 * core
    rs = {}
    for d in (2, 1, 3, 0):
        part[d] = partial_for(d, 1 - core)
        rs[d] = remote(part.at[d], pairin.at[d], r_send.at[d], r_recv.at[d], partner)
        rs[d].start()
    for d in (2, 1, 3, 0):
        mine[d] = partial_for(d, core)
    up = {"tensor": ((chip + near) % 4) * 2 + core}
    down = {"tensor": ((chip + far) % 4) * 2 + core}
    rs[2].wait_recv()
    bsum[0] = (mine[2].astype(F32) + pairin[2].astype(F32)).astype(BF16)
    s2 = remote(bsum.at[0], landed.at[0], s_send.at[0], s_recv.at[0], up)
    s2.start()
    rs[1].wait_recv()
    rs[3].wait_recv()
    bsum[1] = (mine[far].astype(F32) + pairin[far].astype(F32)).astype(BF16)
    s3 = remote(bsum.at[1], landed.at[1], s_send.at[1], s_recv.at[1], down)
    s3.start()
    rs[0].wait_recv()
    nearsum = mine[near].astype(F32) + pairin[near].astype(F32)
    s2.wait_recv()
    relay[...] = (nearsum + landed[0].astype(F32)).astype(BF16)
    s1 = remote(relay, landed.at[2], s_send.at[2], s_recv.at[2], up)
    s1.start()
    total = mine[0].astype(F32) + pairin[0].astype(F32)
    s3.wait_recv()
    total = total + landed[1].astype(F32)
    s1.wait_recv()
    out_ref[...] = (total + landed[2].astype(F32)).astype(BF16)

    for copy in [first[1], first[3], own_x, second, xf[1], xf[2], xf[3], s1, s2, s3]:
        copy.wait_send()
    for s in range(1, 16):
        pages[s].wait_send()
    for s in range(16):
        pagef[s].wait_send()
    for d in range(4):
        rs[d].wait_send()
    newf[0].wait_send()
    for step in range(1, 4):
        @pl.when(seq >= step)
        def _():
            newf[step].wait_send()

        @pl.when(seq + step < 4)
        def _():
            remote(
                fresh.at[core, 0], fresh.at[core, step], n_send.at[step], n_recv.at[step], {"seq": (seq + step) % 4}
            ).wait_send()


def shards(
    span_tokens, q_weight, kv_weight, out_weight, kv_pool, cache_lengths, slot_requests, page_table
):
    group_id = lax.axis_index("group")
    seq_id = lax.axis_index("seq")
    lane = jnp.arange(16, dtype=jnp.int32)
    picked = (slot_requests[:, None] == lane[None, :]).astype(jnp.int32)
    ids = jnp.sum(picked[:, :, None] * page_table[None, :, :], axis=1)
    wanted = jnp.sum(jnp.where(ids // 16 == group_id, ids % 16, 0), axis=1)
    here = (lane == group_id).astype(jnp.int32)
    my_pick = jnp.sum(picked * here[:, None], axis=0)
    my_ids = jnp.sum(my_pick[:, None] * page_table, axis=0)
    place = jnp.sum(jnp.where(my_ids[None, :] // 16 == lane[:, None], lane[None, :], 0), axis=1)
    length = jnp.sum(my_pick * cache_lengths)
    half_dim = HD // 2
    frequency = jnp.power(F32(10000.0), -jnp.arange(half_dim, dtype=F32) / half_dim)
    positions = length + seq_id * 256 + jnp.arange(256, dtype=jnp.int32)
    angles = frequency[:, None] * positions.astype(F32)[None, :]
    smem = pl.BlockSpec(memory_space=pltpu.SMEM)
    vmem = pl.BlockSpec(memory_space=pltpu.VMEM)
    dma = pltpu.SemaphoreType.DMA
    out = pl.pallas_call(
        layer_kernel,
        out_shape=jax.ShapeDtypeStruct((256, 256), BF16),
        in_specs=[smem] * 3 + [vmem] * 7,
        out_specs=vmem,
        scratch_shapes=[
            pltpu.VMEM((2, 4, 256, 256), BF16),
            pltpu.VMEM((15, HD, PAGE), BF16),
            pltpu.VMEM((2, 16, HD, PAGE), BF16),
            pltpu.VMEM((2, 4, HD, 256), BF16),
            pltpu.VMEM((256, 256), F32),
            pltpu.VMEM((HD, 256), F32),
            pltpu.VMEM((4, HD, 256), BF16),
            pltpu.VMEM((4, HD, 256), F32),
            pltpu.VMEM((4, 1, 256), F32),
            pltpu.VMEM((4, 1, 256), F32),
            pltpu.VMEM((1, 256), jnp.int32),
            pltpu.VMEM((4, 256, 256), BF16),
            pltpu.VMEM((4, 256, 256), BF16),
            pltpu.VMEM((4, 256, 256), BF16),
            pltpu.VMEM((2, 256, 256), BF16),
            pltpu.VMEM((3, 256, 256), BF16),
            pltpu.VMEM((256, 256), BF16),
            dma((4,)), dma((4,)), dma((4,)), dma((4,)),
            dma((16,)), dma((16,)), dma((16,)), dma((16,)),
            dma((4,)), dma((4,)), dma((4,)), dma((4,)),
            dma((4,)), dma((4,)), dma((3,)), dma((3,)),
        ],
        compiler_params=pltpu.CompilerParams(
            collective_id=0, has_side_effects=True, vmem_limit_bytes=48 * 1024 * 1024
        ),
    )(
        wanted, place, length.reshape(1), jnp.cos(angles), jnp.sin(angles),
        span_tokens.reshape(256, 256), q_weight, kv_weight.T, out_weight, jnp.swapaxes(kv_pool, 1, 2),
    )
    return out.reshape(1, 256, 256)


def solution(mesh):
    placed = (
        P("group", "seq", "tensor"),
        P(None, "tensor"),
        P(None, "tensor"),
        P("tensor", None),
        P("group", None, "tensor"),
        P(),
        P(),
        P(),
    )
    return jax.shard_map(
        shards, mesh=mesh, in_specs=placed, out_specs=P("group", "seq", "tensor"), check_vma=False
    )
```

time: 121 us -> 65.7 us (0.54)
  the two profiles are of different devices: /device:TPU:24 before, /device:TPU:96 now
where the time goes in v1:
time: 65.7 us; the launch traced here: 65.3 us
  Pallas kernels  54.9 us (84%)
  local copies, waits for them, and re-layouts  5 us (8%)
  other arithmetic  4.75 us (7%)
  between operations  0.71 us (1%)
    pallas_call x1, Pallas kernels, shards(): pl.pallas_call(layer_kernel, out_shape=jax.ShapeDtypeStruct((256, 256), B...  54.9 us
    unnamed x11, local copies, waits for them, and re-layouts  5 us

profile of v1, /device:TPU:96, one launch (start us, length us, event | category | flops | bytes accessed | tf_op | source)
XLA Modules:
  0.0 65.3 jit_solution(15480000346901754302)
XLA Ops:
  0.0 0.0 copy-start.4
  0.0 0.8 %select_reduce_fusion.1 = s32[16]{0:T(128)S(1)} fusion(s32[16]{0:T(128)S(1)} %compare_convert_fusion, s32[16]{0:T(128)} %param.14), kind=kLoop, calls=%fused_computation.14 | loop fusion | flops 752 | bytes 192 | tf_op jit(solution)/shard_map/reduce_sum | solution.py:301
  0.8 1.3 %multiply_reduce_fusion.2 = s32[]{:T(128)} fusion(s32[16]{0:T(128)S(1)} %select_reduce_fusion.1, s32[16]{0:T(128)} %param.13), kind=kLoop, calls=%fused_computation.27 | loop fusion | flops 31 | bytes 132 | tf_op jit(solution)/shard_map/reduce_sum | solution.py:304
  2.7 0.8 %multiply_reduce_fusion.1 = s32[16]{0:T(128)S(1)} fusion(s32[16,16]{1,0:T(8,128)} %param.15, s32[16]{0:T(128)S(1)} %select_reduce_fusion.1), kind=kLoop, calls=%fused_computation.13 | loop fusion | flops 496 | bytes 1152 | tf_op jit(solution)/shard_map/reduce_sum | solution.py:302
  3.6 0.7 %fusion.3 = s32[16,16]{1,0:T(8,128)S(1)} fusion(s32[16]{0:T(128)} %param.14), kind=kLoop, calls=%fused_computation.17 | loop fusion | flops 512 | bytes 1088 | tf_op jit(solution)/shard_map/convert_element_type | solution.py:297
  4.3 0.8 %multiply_reduce_fusion = s32[16,16]{1,0:T(8,128)S(1)} fusion(s32[16,16]{1,0:T(8,128)} %param.15, s32[16,16]{1,0:T(8,128)S(1)} %fusion.3), kind=kLoop, calls=%fused_computation | loop fusion | flops 7936 | bytes 3072 | tf_op jit(solution)/shard_map/reduce_sum | solution.py:298
  5.1 0.1 fusion.2
  5.2 0.2 multiply_sine_fusion
  5.4 0.0 copy-done.4
  5.4 0.0 copy-start
  5.5 1.2 %copy-done = bf16[2048,256]{1,0:T(8,128)(2,1)S(1)} copy-done((bf16[2048,256]{1,0:T(8,128)(2,1)S(1)}, bf16[2048,256]{1,0:T(8,128)(2,1)}, u32[]{:S(2)}) %copy-start) | copy-done | bytes 1048600
  6.7 0.0 copy-start.1
  6.7 1.2 %copy-done.1 = bf16[256,2048]{1,0:T(8,128)(2,1)S(1)} copy-done((bf16[256,2048]{1,0:T(8,128)(2,1)S(1)}, bf16[256,2048]{1,0:T(8,128)(2,1)}, u32[]{:S(2)}) %copy-start.1) | copy-done | bytes 1048600
  7.9 0.0 copy-start.2
  7.9 0.9 %copy-done.2 = bf16[2048,64]{0,1:T(8,128)(2,1)S(1)} copy-done((bf16[2048,64]{0,1:T(8,128)(2,1)S(1)}, bf16[2048,64]{0,1:T(8,128)(2,1)}, u32[]{:S(2)}) %copy-start.2) | copy-done | bytes 262168
  8.8 0.0 copy-start.3
  8.8 0.9 %copy-done.3 = bf16[16,128,64]{1,2,0:T(8,128)(2,1)S(1)} copy-done((bf16[16,128,64]{1,2,0:T(8,128)(2,1)S(1)}, bf16[16,128,64]{1,2,0:T(8,128)(2,1)}, u32[]{:S(2)}) %copy-start.3) | copy-done | bytes 262168
  9.8 54.9 %shard_map.82 = bf16[256,256]{1,0:T(8,128)(2,1)S(1)} custom-call(s32[16]{0:T(128)S(1)} %get-tuple-element.7.wanted_ref, s32[16]{0:T(128)S(1)} %get-tuple-element.8.place_ref, s32[1]{0:T(128)} %bitcast.length_ref, f32[32,256]{1,0:T(8,128)S(1)} %get-tuple-element.6.cos_ref, f32[32,256]{1,0:T(8,128)S(1)} %get-tuple-element.5.sin_ref, ...), custom_call_target="tpu_custom_call" | custom-call | tf_op jit(solution)/shard_map/pallas_call | solution.py:312
  64.7 0.7 %copy.10 = bf16[1,256,256]{2,1,0:T(8,128)(2,1)} copy(bf16[1,256,256]{2,1,0:T(8,128)(2,1)S(1)} %bitcast.5) | data formatting | bytes 262144
  (4 shorter events, 0.0 us)
Async XLA Ops:
  0.0 5.4 %copy-start.4 = (bf16[1,256,256]{2,1,0:T(8,128)(2,1)S(1)}, bf16[1,256,256]{2,1,0:T(8,128)(2,1)}, u32[]{:S(2)}) copy-start(bf16[1,256,256]{2,1,0:T(8,128)(2,1)} %param.8) | copy-start | bytes 393220
  5.4 1.2 %copy-start = (bf16[2048,256]{1,0:T(8,128)(2,1)S(1)}, bf16[2048,256]{1,0:T(8,128)(2,1)}, u32[]{:S(2)}) copy-start(bf16[2048,256]{1,0:T(8,128)(2,1)} %qw_ref.1) | copy-start | bytes 3145732
  6.7 1.2 %copy-start.1 = (bf16[256,2048]{1,0:T(8,128)(2,1)S(1)}, bf16[256,2048]{1,0:T(8,128)(2,1)}, u32[]{:S(2)}) copy-start(bf16[256,2048]{1,0:T(8,128)(2,1)} %ow_ref.1) | copy-start | bytes 3145732
  7.9 0.9 %copy-start.2 = (bf16[2048,64]{0,1:T(8,128)(2,1)S(1)}, bf16[2048,64]{0,1:T(8,128)(2,1)}, u32[]{:S(2)}) copy-start(bf16[2048,64]{0,1:T(8,128)(2,1)} %param.10) | copy-start | bytes 786436
  8.8 0.9 %copy-start.3 = (bf16[16,128,64]{1,2,0:T(8,128)(2,1)S(1)}, bf16[16,128,64]{1,2,0:T(8,128)(2,1)}, u32[]{:S(2)}) copy-start(bf16[16,128,64]{1,2,0:T(8,128)(2,1)} %param.12) | copy-start | bytes 786436

commit v2 on v1

--- a/solution.py
+++ b/solution.py
@@ -18,9 +18,9 @@
 
 
 def layer_kernel(
-    wanted_ref, place_ref, length_ref, cos_ref, sin_ref, x_ref, qw_ref, kvw_ref, ow_ref, pool_ref,
+    slots_ref, lengths_ref, table_ref, freq_ref, x_hbm, qw_hbm, kvw_hbm, ow_hbm, pool_hbm,
     out_ref,
-    xs, outp, kv, fresh, qacc, kvacc, qt, acc, top, tot, thr_ref, part, mine, pairin, bsum, landed, relay,
+    x_ref, qw_ref, kvw_ref, ow_ref, pool_ref, place_ref, load_sem, xs, outp, kv, fresh, qacc, kvacc, qt, acc, top, tot, thr_ref, cos_ref, sin_ref, part, mine, pairin, bsum, landed, relay,
     x_send, x_recv, xf_send, xf_recv, p_send, p_recv, pf_send, pf_recv,
     n_send, n_recv, nf_send, nf_recv, r_send, r_recv, s_send, s_recv,
 ):
@@ -64,17 +64,57 @@
             pl.semaphore_signal(barrier, inc=1, device_id=chip_at(d), device_id_type=MESH)
     pl.semaphore_signal(barrier, inc=1, device_id=partner, device_id_type=MESH)
 
-    for s in range(1, 16):
-        outp[s - 1] = pool_ref[wanted_ref[group_to(s)]]
-    kv[core, 0] = pool_ref[wanted_ref[group]]
+    loads = [
+        pltpu.make_async_copy(src, dst, load_sem.at[i])
+        for i, (src, dst) in enumerate(
+            [(pool_hbm, pool_ref), (x_hbm, x_ref), (qw_hbm, qw_ref), (kvw_hbm, kvw_ref), (ow_hbm, ow_ref)]
+        )
+    ]
+    for copy in loads:
+        copy.start()
+
+    mine_req = slots_ref[group]
+    length = lengths_ref[mine_req]
+    my_ids = [table_ref[mine_req, w] for w in range(16)]
+
+    def find_place(s, carry):
+        low = group_from(s) * 16
+        at = 0
+        for w in range(16):
+            off = my_ids[w] - low
+            at = at + jnp.where((off >= 0) & (off < 16), w, 0)
+        place_ref[s] = at
+        return carry
+
+    lax.fori_loop(0, 16, find_place, 0)
+    loads[0].wait()
+
+    def pick(s, carry):
+        req = slots_ref[group_to(s)]
+        at = 0
+        for w in range(16):
+            off = table_ref[req, w] - group * 16
+            at = at + jnp.where((off >= 0) & (off < 16), off, 0)
+        outp[s] = pool_ref[at]
+        return carry
+
+    lax.fori_loop(0, 16, pick, 0)
+    kv[core, 0] = outp[0]
+    at_pos = lax.broadcasted_iota(jnp.int32, (32, 256), 1) + (length + seq * 256)
+    angles = at_pos.astype(F32) * freq_ref[...]
+    cos = jnp.cos(angles)
+    sin = jnp.sin(angles)
+    cos_ref[...] = cos
+    sin_ref[...] = sin
     thr_ref[...] = jnp.maximum(
-        lax.broadcasted_iota(jnp.int32, (1, 256), 1) + seq * 256, WINDOW - 1 - length_ref[0]
+        lax.broadcasted_iota(jnp.int32, (1, 256), 1) + seq * 256, WINDOW - 1 - length
     )
     for h in range(4):
         acc[h] = jnp.zeros((HD, 256), F32)
         top[h] = jnp.full((1, 256), FLOOR, F32)
         tot[h] = jnp.zeros((1, 256), F32)
 
+    loads[1].wait()
     pl.semaphore_wait(barrier, 21)
 
     first = {d: remote(x_ref, xs.at[0, 4 - d], x_send.at[d], x_recv.at[4 - d], chip_at(d)) for d in (1, 3)}
@@ -84,7 +124,7 @@
     own_x.start()
     order = [1, 3, 4, 8, 12, 5, 7, 9, 11, 13, 15, 2, 6, 10, 14]
     pages = {
-        s: remote(outp.at[s - 1], kv.at[core, s], p_send.at[s], p_recv.at[s], page_dev(s)) for s in order
+        s: remote(outp.at[s], kv.at[core, s], p_send.at[s], p_recv.at[s], page_dev(s)) for s in order
     }
     for s in (2, 6, 10, 14, 1, 3, 5, 7, 9, 11, 13, 15, 4, 8, 12):
         pages[s].start()
@@ -92,6 +132,8 @@
         s: remote(kv.at[core, s], kv.at[core, s], pf_send.at[s], pf_recv.at[s], partner) for s in range(16)
     }
     pagef[0].start()
+    loads[2].wait()
+    loads[3].wait()
 
     def project(p, d):
         block = x_ref[...] if (p, d) == (0, 0) else xs[p, d]
@@ -177,7 +219,7 @@
         def mask(s):
             pieces = []
             for i, slot in enumerate(slots):
-                low = thr_ref[...] - place_ref[group_from(slot)] * PAGE
+                low = thr_ref[...] - place_ref[slot] * PAGE
                 pieces.append(jnp.where(row > low, s[i * PAGE:(i + 1) * PAGE], NEG))
             return jnp.concatenate(pieces, axis=0)
 
@@ -229,6 +271,7 @@
             new_ready(step)
             fold(fresh[0, step], fresh[1, step], lambda s: s)
 
+    loads[4].wait()
     heads = jnp.concatenate([(acc[h] / tot[h]).T.astype(BF16) for h in range(4)], axis=1)
 
     def partial_for(d, c):
@@ -291,32 +334,28 @@
 def shards(
     span_tokens, q_weight, kv_weight, out_weight, kv_pool, cache_lengths, slot_requests, page_table
 ):
-    group_id = lax.axis_index("group")
-    seq_id = lax.axis_index("seq")
-    lane = jnp.arange(16, dtype=jnp.int32)
-    picked = (slot_requests[:, None] == lane[None, :]).astype(jnp.int32)
-    ids = jnp.sum(picked[:, :, None] * page_table[None, :, :], axis=1)
-    wanted = jnp.sum(jnp.where(ids // 16 == group_id, ids % 16, 0), axis=1)
-    here = (lane == group_id).astype(jnp.int32)
-    my_pick = jnp.sum(picked * here[:, None], axis=0)
-    my_ids = jnp.sum(my_pick[:, None] * page_table, axis=0)
-    place = jnp.sum(jnp.where(my_ids[None, :] // 16 == lane[:, None], lane[None, :], 0), axis=1)
-    length = jnp.sum(my_pick * cache_lengths)
     half_dim = HD // 2
     frequency = jnp.power(F32(10000.0), -jnp.arange(half_dim, dtype=F32) / half_dim)
-    positions = length + seq_id * 256 + jnp.arange(256, dtype=jnp.int32)
-    angles = frequency[:, None] * positions.astype(F32)[None, :]
+    frequency = jnp.broadcast_to(frequency[:, None], (half_dim, 256))
     smem = pl.BlockSpec(memory_space=pltpu.SMEM)
     vmem = pl.BlockSpec(memory_space=pltpu.VMEM)
+    hbm = pl.BlockSpec(memory_space=pl.ANY)
     dma = pltpu.SemaphoreType.DMA
     out = pl.pallas_call(
         layer_kernel,
         out_shape=jax.ShapeDtypeStruct((256, 256), BF16),
-        in_specs=[smem] * 3 + [vmem] * 7,
+        in_specs=[smem] * 3 + [vmem] + [hbm] * 5,
         out_specs=vmem,
         scratch_shapes=[
+            pltpu.VMEM((256, 256), BF16),
+            pltpu.VMEM((2048, 256), BF16),
+            pltpu.VMEM((HD, 2048), BF16),
+            pltpu.VMEM((256, 2048), BF16),
+            pltpu.VMEM((16, HD, PAGE), BF16),
+            pltpu.SMEM((16,), jnp.int32),
+            dma((5,)),
             pltpu.VMEM((2, 4, 256, 256), BF16),
-            pltpu.VMEM((15, HD, PAGE), BF16),
+            pltpu.VMEM((16, HD, PAGE), BF16),
             pltpu.VMEM((2, 16, HD, PAGE), BF16),
             pltpu.VMEM((2, 4, HD, 256), BF16),
             pltpu.VMEM((256, 256), F32),
@@ -326,6 +365,8 @@
             pltpu.VMEM((4, 1, 256), F32),
             pltpu.VMEM((4, 1, 256), F32),
             pltpu.VMEM((1, 256), jnp.int32),
+            pltpu.VMEM((32, 256), F32),
+            pltpu.VMEM((32, 256), F32),
             pltpu.VMEM((4, 256, 256), BF16),
             pltpu.VMEM((4, 256, 256), BF16),
             pltpu.VMEM((4, 256, 256), BF16),
@@ -338,10 +379,10 @@
             dma((4,)), dma((4,)), dma((3,)), dma((3,)),
         ],
         compiler_params=pltpu.CompilerParams(
-            collective_id=0, has_side_effects=True, vmem_limit_bytes=48 * 1024 * 1024
+            collective_id=0, has_side_effects=True, vmem_limit_bytes=63 * 1024 * 1024
         ),
     )(
-        wanted, place, length.reshape(1), jnp.cos(angles), jnp.sin(angles),
+        slot_requests, cache_lengths, page_table, frequency,
         span_tokens.reshape(256, 256), q_weight, kv_weight.T, out_weight, jnp.swapaxes(kv_pool, 1, 2),
     )
     return out.reshape(1, 256, 256)

time: 65.7 us -> 57.7 us (0.88)
  other arithmetic: 4.75 us -> 0.01 us
  local copies, waits for them, and re-layouts: 5 us -> 2.26 us
  between operations: 0.71 us -> 0.01 us
    reduce_sum x5 -> x0, other arithmetic: 3.79 us -> none  [the longest x1 1.29 us: shards(): length = jnp.sum(my_pick * cache_lengths)]
    unnamed x11 -> x1, local copies, waits for them, and re-layouts: 5 us -> 1.57 us
    convert_element_type x3 -> x0, other arithmetic: 0.74 us -> none  [the longest x1 0.73 us: shards(): picked = (slot_requests[:, None] == lane[None, :]).astype(jnp.int32)]
    broadcast_in_dim x0 -> x1, local copies, waits for them, and re-layouts: none -> 0.69 us  [shards(): frequency = jnp.broadcast_to(frequency[:, None], (half_dim, 256))]
where the time goes in v2:
time: 57.7 us; the launch traced here: 57.5 us
  Pallas kernels  55.2 us (96%)
  local copies, waits for them, and re-layouts  2.26 us (4%)
    pallas_call x1, Pallas kernels, shards(): pl.pallas_call(layer_kernel, out_shape=jax.ShapeDtypeStruct((256, 256), B...  55.2 us
    unnamed x1, local copies, waits for them, and re-layouts  1.57 us

profile of v2, /device:TPU:96, one launch (start us, length us, event | category | flops | bytes accessed | tf_op | source)
XLA Modules:
  0.0 57.5 jit_solution(14114975043573991876)
XLA Ops:
  0.0 0.7 %broadcast_in_dim.2.freq_ref = f32[32,256]{1,0:T(8,128)} broadcast(f32[32]{0:T(128)S(1)} %multiply_power_fusion), dimensions={0} | broadcast | bytes 32896 | tf_op jit(solution)/shard_map/broadcast_in_dim | solution.py:339
  0.7 55.2 %shard_map.82 = bf16[256,256]{1,0:T(8,128)(2,1)} custom-call(s32[16]{0:T(128)} %slots_ref.1, s32[16]{0:T(128)} %lengths_ref.1, s32[16,16]{1,0:T(8,128)} %table_ref.1, f32[32,256]{1,0:T(8,128)} %broadcast_in_dim.2.freq_ref, bf16[256,256]{1,0:T(8,128)(2,1)} %bitcast.7, bf16[2048,256]{1,0:T(8,128)(2,1)} %qw_hbm.1, bf16[64,2048]{1,0:T(8,128)(2,1)} %bitcast.5, ...), custom_call_target="tpu_custom_call" | custom-call | tf_op jit(solution)/shard_map/pallas_call | solution.py:344
  55.9 1.6 %copy.10 = bf16[1,256,256]{2,1,0:T(8,128)(2,1)} copy(bf16[1,256,256]{2,1,0:T(8,128)(2,1)} %bitcast.4) | data formatting | bytes 262144
  (1 shorter events, 0.0 us)

commit v3 on v2

--- a/solution.py
+++ b/solution.py
@@ -1,7 +1,6 @@
-import functools
-
 import jax
 import jax.numpy as jnp
+import numpy as np
 from jax import lax
 from jax.experimental import pallas as pl
 from jax.experimental.pallas import tpu as pltpu
@@ -75,18 +74,6 @@
 
     mine_req = slots_ref[group]
     length = lengths_ref[mine_req]
-    my_ids = [table_ref[mine_req, w] for w in range(16)]
-
-    def find_place(s, carry):
-        low = group_from(s) * 16
-        at = 0
-        for w in range(16):
-            off = my_ids[w] - low
-            at = at + jnp.where((off >= 0) & (off < 16), w, 0)
-        place_ref[s] = at
-        return carry
-
-    lax.fori_loop(0, 16, find_place, 0)
     loads[0].wait()
 
     def pick(s, carry):
@@ -100,20 +87,6 @@
 
     lax.fori_loop(0, 16, pick, 0)
     kv[core, 0] = outp[0]
-    at_pos = lax.broadcasted_iota(jnp.int32, (32, 256), 1) + (length + seq * 256)
-    angles = at_pos.astype(F32) * freq_ref[...]
-    cos = jnp.cos(angles)
-    sin = jnp.sin(angles)
-    cos_ref[...] = cos
-    sin_ref[...] = sin
-    thr_ref[...] = jnp.maximum(
-        lax.broadcasted_iota(jnp.int32, (1, 256), 1) + seq * 256, WINDOW - 1 - length
-    )
-    for h in range(4):
-        acc[h] = jnp.zeros((HD, 256), F32)
-        top[h] = jnp.full((1, 256), FLOOR, F32)
-        tot[h] = jnp.zeros((1, 256), F32)
-
     loads[1].wait()
     pl.semaphore_wait(barrier, 21)
 
@@ -132,6 +105,34 @@
         s: remote(kv.at[core, s], kv.at[core, s], pf_send.at[s], pf_recv.at[s], partner) for s in range(16)
     }
     pagef[0].start()
+
+    at_pos = lax.broadcasted_iota(jnp.int32, (32, 256), 1) + (length + seq * 256)
+    angles = at_pos.astype(F32) * freq_ref[...]
+    cos = jnp.cos(angles)
+    sin = jnp.sin(angles)
+    cos_ref[...] = cos
+    sin_ref[...] = sin
+    thr_ref[...] = jnp.maximum(
+        lax.broadcasted_iota(jnp.int32, (1, 256), 1) + seq * 256, WINDOW - 1 - length
+    )
+    for h in range(4):
+        acc[h] = jnp.zeros((HD, 256), F32)
+        top[h] = jnp.full((1, 256), FLOOR, F32)
+        tot[h] = jnp.zeros((1, 256), F32)
+
+    my_ids = [table_ref[mine_req, w] for w in range(16)]
+
+    def find_place(s, carry):
+        low = group_from(s) * 16
+        at = 0
+        for w in range(16):
+            off = my_ids[w] - low
+            at = at + jnp.where((off >= 0) & (off < 16), w, 0)
+        place_ref[s] = at
+        return carry
+
+    lax.fori_loop(0, 16, find_place, 0)
+
     loads[2].wait()
     loads[3].wait()
 
@@ -199,19 +200,21 @@
     def fold(keys, values, mask):
         kb = keys.T
 
-        def head(h, carry):
-            s = jnp.dot(kb, qt[h], preferred_element_type=F32)
-            s = mask(s)
-            old = top[h]
-            new = jnp.maximum(old, jnp.max(s, axis=0, keepdims=True))
-            p = jnp.exp(s - new)
-            alpha = jnp.exp(old - new)
-            top[h] = new
-            tot[h] = tot[h] * alpha + jnp.sum(p, axis=0, keepdims=True)
-            acc[h] = acc[h] * alpha + jnp.dot(values, p.astype(BF16), preferred_element_type=F32)
+        def head_pair(i, carry):
+            scores = [jnp.dot(kb, qt[2 * i + k], preferred_element_type=F32) for k in range(2)]
+            for k in range(2):
+                h = 2 * i + k
+                s = mask(scores[k])
+                old = top[h]
+                new = jnp.maximum(old, jnp.max(s, axis=0, keepdims=True))
+                p = jnp.exp(s - new)
+                alpha = jnp.exp(old - new)
+                top[h] = new
+                tot[h] = tot[h] * alpha + jnp.sum(p, axis=0, keepdims=True)
+                acc[h] = acc[h] * alpha + jnp.dot(values, p.astype(BF16), preferred_element_type=F32)
             return carry
 
-        lax.fori_loop(0, 4, head, 0)
+        lax.fori_loop(0, 2, head_pair, 0)
 
     row = lax.broadcasted_iota(jnp.int32, (PAGE, 256), 0)
 
@@ -280,37 +283,44 @@
 
     near = 1 + 2 * core
     far = 3 - 2 * core
+    up = {"tensor": ((chip + near) % 4) * 2 + core}
+    down = {"tensor": ((chip + far) % 4) * 2 + core}
+    halves = [pl.ds(0, 128), pl.ds(128, 128)]
     rs = {}
     for d in (2, 1, 3, 0):
         part[d] = partial_for(d, 1 - core)
         rs[d] = remote(part.at[d], pairin.at[d], r_send.at[d], r_recv.at[d], partner)
         rs[d].start()
-    for d in (2, 1, 3, 0):
-        mine[d] = partial_for(d, core)
-    up = {"tensor": ((chip + near) % 4) * 2 + core}
-    down = {"tensor": ((chip + far) % 4) * 2 + core}
+        if d == 2:
+            mine[2] = partial_for(2, core)
     rs[2].wait_recv()
-    bsum[0] = (mine[2].astype(F32) + pairin[2].astype(F32)).astype(BF16)
-    s2 = remote(bsum.at[0], landed.at[0], s_send.at[0], s_recv.at[0], up)
-    s2.start()
+    s2, s1 = [], []
+    for i, half in enumerate(halves):
+        bsum[0, half] = (mine[2, half].astype(F32) + pairin[2, half].astype(F32)).astype(BF16)
+        s2.append(remote(bsum.at[0, half], landed.at[0, half], s_send.at[i], s_recv.at[i], up))
+        s2[i].start()
+    mine[1] = partial_for(1, core)
+    mine[3] = partial_for(3, core)
     rs[1].wait_recv()
     rs[3].wait_recv()
     bsum[1] = (mine[far].astype(F32) + pairin[far].astype(F32)).astype(BF16)
-    s3 = remote(bsum.at[1], landed.at[1], s_send.at[1], s_recv.at[1], down)
+    s3 = remote(bsum.at[1], landed.at[1], s_send.at[2], s_recv.at[2], down)
     s3.start()
+    mine[0] = partial_for(0, core)
+    for i, half in enumerate(halves):
+        nearsum = mine[near, half].astype(F32) + pairin[near, half].astype(F32)
+        s2[i].wait_recv()
+        relay[half] = (nearsum + landed[0, half].astype(F32)).astype(BF16)
+        s1.append(remote(relay.at[half], landed.at[2, half], s_send.at[3 + i], s_recv.at[3 + i], up))
+        s1[i].start()
     rs[0].wait_recv()
-    nearsum = mine[near].astype(F32) + pairin[near].astype(F32)
-    s2.wait_recv()
-    relay[...] = (nearsum + landed[0].astype(F32)).astype(BF16)
-    s1 = remote(relay, landed.at[2], s_send.at[2], s_recv.at[2], up)
-    s1.start()
-    total = mine[0].astype(F32) + pairin[0].astype(F32)
     s3.wait_recv()
-    total = total + landed[1].astype(F32)
-    s1.wait_recv()
-    out_ref[...] = (total + landed[2].astype(F32)).astype(BF16)
-
-    for copy in [first[1], first[3], own_x, second, xf[1], xf[2], xf[3], s1, s2, s3]:
+    for i, half in enumerate(halves):
+        total = mine[0, half].astype(F32) + pairin[0, half].astype(F32) + landed[1, half].astype(F32)
+        s1[i].wait_recv()
+        out_ref[half] = (total + landed[2, half].astype(F32)).astype(BF16)
+
+    for copy in [first[1], first[3], own_x, second, xf[1], xf[2], xf[3], *s1, *s2, s3]:
         copy.wait_send()
     for s in range(1, 16):
         pages[s].wait_send()
@@ -335,8 +345,8 @@
     span_tokens, q_weight, kv_weight, out_weight, kv_pool, cache_lengths, slot_requests, page_table
 ):
     half_dim = HD // 2
-    frequency = jnp.power(F32(10000.0), -jnp.arange(half_dim, dtype=F32) / half_dim)
-    frequency = jnp.broadcast_to(frequency[:, None], (half_dim, 256))
+    frequency = np.power(10000.0, -np.arange(half_dim) / half_dim).astype(np.float32)
+    frequency = jnp.asarray(np.repeat(frequency[:, None], 256, axis=1))
     smem = pl.BlockSpec(memory_space=pltpu.SMEM)
     vmem = pl.BlockSpec(memory_space=pltpu.VMEM)
     hbm = pl.BlockSpec(memory_space=pl.ANY)
@@ -376,7 +386,7 @@
             dma((4,)), dma((4,)), dma((4,)), dma((4,)),
             dma((16,)), dma((16,)), dma((16,)), dma((16,)),
             dma((4,)), dma((4,)), dma((4,)), dma((4,)),
-            dma((4,)), dma((4,)), dma((3,)), dma((3,)),
+            dma((4,)), dma((4,)), dma((5,)), dma((5,)),
         ],
         compiler_params=pltpu.CompilerParams(
             collective_id=0, has_side_effects=True, vmem_limit_bytes=63 * 1024 * 1024

time: 57.7 us -> 51.6 us (0.89)
  the two profiles are of different devices: /device:TPU:96 before, /device:TPU:2 now
where the time goes in v3:
time: 51.6 us; the launch traced here: 51.4 us
  Pallas kernels  49.9 us (97%)
  local copies, waits for them, and re-layouts  1.57 us (3%)
    pallas_call x1, Pallas kernels, shards(): pl.pallas_call(layer_kernel, out_shape=jax.ShapeDtypeStruct((256, 256), B...  49.9 us
    unnamed x1, local copies, waits for them, and re-layouts  1.57 us

profile of v3, /device:TPU:2, one launch (start us, length us, event | category | flops | bytes accessed | tf_op | source)
XLA Modules:
  0.0 51.4 jit_solution(2502929097635452359)
XLA Ops:
  0.0 49.9 %shard_map.91 = bf16[256,256]{1,0:T(8,128)(2,1)} custom-call(s32[16]{0:T(128)} %slots_ref.1, s32[16]{0:T(128)} %lengths_ref.1, s32[16,16]{1,0:T(8,128)} %table_ref.1, f32[32,256]{1,0:T(8,128)} %constant.2.clone.freq_ref, bf16[256,256]{1,0:T(8,128)(2,1)} %bitcast.7, bf16[2048,256]{1,0:T(8,128)(2,1)} %qw_hbm.1, bf16[64,2048]{1,0:T(8,128)(2,1)} %bitcast.5, ...), custom_call_target="tpu_custom_call" | custom-call | tf_op jit(solution)/shard_map/pallas_call | solution.py:354
  49.9 1.6 %copy.11 = bf16[1,256,256]{2,1,0:T(8,128)(2,1)} copy(bf16[1,256,256]{2,1,0:T(8,128)(2,1)} %bitcast.4) | data formatting | bytes 262144

commit v4 on v3

--- a/solution.py
+++ b/solution.py
@@ -17,9 +17,9 @@
 
 
 def layer_kernel(
-    slots_ref, lengths_ref, table_ref, freq_ref, x_hbm, qw_hbm, kvw_hbm, ow_hbm, pool_hbm,
+    slots_ref, lengths_ref, table_ref, freq_hbm, x_hbm, qw_hbm, kvw_hbm, ow_hbm, pool_hbm,
     out_ref,
-    x_ref, qw_ref, kvw_ref, ow_ref, pool_ref, place_ref, load_sem, xs, outp, kv, fresh, qacc, kvacc, qt, acc, top, tot, thr_ref, cos_ref, sin_ref, part, mine, pairin, bsum, landed, relay,
+    x_ref, qw_ref, kvw_ref, ow_ref, pool_ref, freq_ref, place_ref, load_sem, xs, outp, kv, fresh, qacc, kvacc, qt, acc, top, tot, thr_ref, cos_ref, sin_ref, part, mine, pairin, bsum, landed, relay,
     x_send, x_recv, xf_send, xf_recv, p_send, p_recv, pf_send, pf_recv,
     n_send, n_recv, nf_send, nf_recv, r_send, r_recv, s_send, s_recv,
 ):
@@ -66,7 +66,7 @@
     loads = [
         pltpu.make_async_copy(src, dst, load_sem.at[i])
         for i, (src, dst) in enumerate(
-            [(pool_hbm, pool_ref), (x_hbm, x_ref), (qw_hbm, qw_ref), (kvw_hbm, kvw_ref), (ow_hbm, ow_ref)]
+            [(pool_hbm, pool_ref), (x_hbm, x_ref), (qw_hbm, qw_ref), (kvw_hbm, kvw_ref), (ow_hbm, ow_ref), (freq_hbm, freq_ref)]
         )
     ]
     for copy in loads:
@@ -81,7 +81,7 @@
         at = 0
         for w in range(16):
             off = table_ref[req, w] - group * 16
-            at = at + jnp.where((off >= 0) & (off < 16), off, 0)
+            at = at + jnp.where((off & -16) == 0, off, 0)
         outp[s] = pool_ref[at]
         return carry
 
@@ -90,10 +90,17 @@
     loads[1].wait()
     pl.semaphore_wait(barrier, 21)
 
-    first = {d: remote(x_ref, xs.at[0, 4 - d], x_send.at[d], x_recv.at[4 - d], chip_at(d)) for d in (1, 3)}
+    fwd = 1 + 2 * core
+    back = 3 - 2 * core
+    halves = [pl.ds(0, 128), pl.ds(128, 128)]
+    first = [
+        remote(x_ref.at[half], xs.at[0, back, half], x_send.at[i], x_recv.at[i], chip_at(fwd))
+        for i, half in enumerate(halves)
+    ]
+    first.append(remote(x_ref, xs.at[0, fwd], x_send.at[2], x_recv.at[2], chip_at(back)))
     own_x = remote(x_ref, xs.at[1, 0], xf_send.at[0], xf_recv.at[0], partner)
-    for d in (1, 3):
-        first[d].start()
+    for copy in first:
+        copy.start()
     own_x.start()
     order = [1, 3, 4, 8, 12, 5, 7, 9, 11, 13, 15, 2, 6, 10, 14]
     pages = {
@@ -106,6 +113,7 @@
     }
     pagef[0].start()
 
+    loads[5].wait()
     at_pos = lax.broadcasted_iota(jnp.int32, (32, 256), 1) + (length + seq * 256)
     angles = at_pos.astype(F32) * freq_ref[...]
     cos = jnp.cos(angles)
@@ -127,7 +135,7 @@
         at = 0
         for w in range(16):
             off = my_ids[w] - low
-            at = at + jnp.where((off >= 0) & (off < 16), w, 0)
+            at = at + jnp.where((off & -16) == 0, w, 0)
         place_ref[s] = at
         return carry
 
@@ -136,38 +144,44 @@
     loads[2].wait()
     loads[3].wait()
 
-    def project(p, d):
-        block = x_ref[...] if (p, d) == (0, 0) else xs[p, d]
+    def project(p, d, start=False):
+        block = x_ref[...] if start else xs[p, d]
         t = ((chip + d) % 4) * 2 + (core if p == 0 else 1 - core)
         rows = pl.ds(pl.multiple_of(t * 256, 256), 256)
         q = jnp.dot(block, qw_ref[rows, :], preferred_element_type=F32)
         f = lax.dot_general(kvw_ref[:, rows], block, (((1,), (1,)), ((), ())), preferred_element_type=F32)
-        if (p, d) == (0, 0):
+        if start:
             qacc[...] = q
             kvacc[...] = f
         else:
             qacc[...] += q
             kvacc[...] += f
 
-    project(0, 0)
-    xf = {d: remote(xs.at[0, d], xs.at[1, d], xf_send.at[d], xf_recv.at[d], partner) for d in (1, 2, 3)}
-    from_slot = 3 - 2 * core
-    on = {"tensor": ((chip + 1 + 2 * core) % 4) * 2 + core}
-    first[3].wait_recv()
-    first[1].wait_recv()
-    second = remote(xs.at[0, from_slot], xs.at[0, 2], x_send.at[2], x_recv.at[2], on)
-    second.start()
-    xf[1].start()
-    xf[3].start()
+    def hand_over(i, d):
+        return remote(xs.at[0, d], xs.at[1, d], xf_send.at[i], xf_recv.at[i], partner)
+
+    project(0, 0, True)
+    second = []
+    for i, half in enumerate(halves):
+        first[i].wait_recv()
+        second.append(
+            remote(xs.at[0, back, half], xs.at[0, 2, half], x_send.at[3 + i], x_recv.at[3 + i], chip_at(fwd))
+        )
+        second[i].start()
+    xf = [hand_over(1, back), hand_over(3, fwd), hand_over(2, 2)]
+    xf[0].start()
     own_x.wait_recv()
     project(1, 0)
-    project(0, 1)
-    project(0, 3)
-    xf[1].wait_recv()
-    project(1, 1)
-    xf[3].wait_recv()
-    project(1, 3)
-    second.wait_recv()
+    project(0, back)
+    first[2].wait_recv()
+    xf[1].start()
+    project(0, fwd)
+    hand_over(1, fwd).wait_recv()
+    project(1, fwd)
+    hand_over(3, back).wait_recv()
+    project(1, back)
+    second[0].wait_recv()
+    second[1].wait_recv()
     xf[2].start()
     project(0, 2)
     xf[2].wait_recv()
@@ -246,13 +260,13 @@
     def new_ready(i):
         remote(fresh.at[core, i], fresh.at[1 - core, i], nf_send.at[i], nf_recv.at[i], partner).wait_recv()
 
+    take([4, 8, 12])
     new_ready(0)
     fold(fresh[0, 0], fresh[1, 0], lambda s: jnp.where(causal, s, NEG))
     c0, c1, c2, c3 = [0, 4, 8, 12], [1, 3, 5, 7], [9, 11, 13, 15], [2, 6, 10, 14]
-    take(c0[1:])
-    take(c1)
     ready(c0)
     fold_pages(c0)
+    take(c1)
     take(c2)
     ready(c1)
     fold_pages(c1)
@@ -285,7 +299,6 @@
     far = 3 - 2 * core
     up = {"tensor": ((chip + near) % 4) * 2 + core}
     down = {"tensor": ((chip + far) % 4) * 2 + core}
-    halves = [pl.ds(0, 128), pl.ds(128, 128)]
     rs = {}
     for d in (2, 1, 3, 0):
         part[d] = partial_for(d, 1 - core)
@@ -320,7 +333,7 @@
         s1[i].wait_recv()
         out_ref[half] = (total + landed[2, half].astype(F32)).astype(BF16)
 
-    for copy in [first[1], first[3], own_x, second, xf[1], xf[2], xf[3], *s1, *s2, s3]:
+    for copy in [*first, own_x, *second, *xf, *s1, *s2, s3]:
         copy.wait_send()
     for s in range(1, 16):
         pages[s].wait_send()
@@ -354,7 +367,7 @@
     out = pl.pallas_call(
         layer_kernel,
         out_shape=jax.ShapeDtypeStruct((256, 256), BF16),
-        in_specs=[smem] * 3 + [vmem] + [hbm] * 5,
+        in_specs=[smem] * 3 + [hbm] * 6,
         out_specs=vmem,
         scratch_shapes=[
             pltpu.VMEM((256, 256), BF16),
@@ -362,8 +375,9 @@
             pltpu.VMEM((HD, 2048), BF16),
             pltpu.VMEM((256, 2048), BF16),
             pltpu.VMEM((16, HD, PAGE), BF16),
+            pltpu.VMEM((32, 256), F32),
             pltpu.SMEM((16,), jnp.int32),
-            dma((5,)),
+            dma((6,)),
             pltpu.VMEM((2, 4, 256, 256), BF16),
             pltpu.VMEM((16, HD, PAGE), BF16),
             pltpu.VMEM((2, 16, HD, PAGE), BF16),
@@ -383,7 +397,7 @@
             pltpu.VMEM((2, 256, 256), BF16),
             pltpu.VMEM((3, 256, 256), BF16),
             pltpu.VMEM((256, 256), BF16),
-            dma((4,)), dma((4,)), dma((4,)), dma((4,)),
+            dma((5,)), dma((5,)), dma((4,)), dma((4,)),
             dma((16,)), dma((16,)), dma((16,)), dma((16,)),
             dma((4,)), dma((4,)), dma((4,)), dma((4,)),
             dma((4,)), dma((4,)), dma((5,)), dma((5,)),

time: 51.6 us -> 51.6 us (level)
  no operation moved by 1% of the time
where the time goes in v4:
time: 51.6 us; the launch traced here: 51.4 us
  Pallas kernels  49.8 us (97%)
  local copies, waits for them, and re-layouts  1.57 us (3%)
    pallas_call x1, Pallas kernels, shards(): pl.pallas_call(layer_kernel, out_shape=jax.ShapeDtypeStruct((256, 256), B...  49.8 us
    unnamed x1, local copies, waits for them, and re-layouts  1.57 us

profile of v4, /device:TPU:2, one launch (start us, length us, event | category | flops | bytes accessed | tf_op | source)
XLA Modules:
  0.0 51.4 jit_solution(14987185343905935156)
XLA Ops:
  0.0 49.8 %shard_map.91 = bf16[256,256]{1,0:T(8,128)(2,1)} custom-call(s32[16]{0:T(128)} %slots_ref.1, s32[16]{0:T(128)} %lengths_ref.1, s32[16,16]{1,0:T(8,128)} %table_ref.1, f32[32,256]{1,0:T(8,128)} %constant.2.clone.freq_hbm, bf16[256,256]{1,0:T(8,128)(2,1)} %bitcast.7, bf16[2048,256]{1,0:T(8,128)(2,1)} %qw_hbm.1, bf16[64,2048]{1,0:T(8,128)(2,1)} %bitcast.5, ...), custom_call_target="tpu_custom_call" | custom-call | tf_op jit(solution)/shard_map/pallas_call | solution.py:367
  49.8 1.6 %copy.11 = bf16[1,256,256]{2,1,0:T(8,128)(2,1)} copy(bf16[1,256,256]{2,1,0:T(8,128)(2,1)} %bitcast.4) | data formatting | bytes 262144

commit v5 on v4

--- a/solution.py
+++ b/solution.py
@@ -20,7 +20,7 @@
     slots_ref, lengths_ref, table_ref, freq_hbm, x_hbm, qw_hbm, kvw_hbm, ow_hbm, pool_hbm,
     out_ref,
     x_ref, qw_ref, kvw_ref, ow_ref, pool_ref, freq_ref, place_ref, load_sem, xs, outp, kv, fresh, qacc, kvacc, qt, acc, top, tot, thr_ref, cos_ref, sin_ref, part, mine, pairin, bsum, landed, relay,
-    x_send, x_recv, xf_send, xf_recv, p_send, p_recv, pf_send, pf_recv,
+    x_send, x_recv, xf_send, xf_recv, p_send, p_recv, z_send, z_recv, pf_send, pf_recv,
     n_send, n_recv, nf_send, nf_recv, r_send, r_recv, s_send, s_recv,
 ):
     group = lax.axis_index("group")
@@ -102,16 +102,29 @@
     for copy in first:
         copy.start()
     own_x.start()
-    order = [1, 3, 4, 8, 12, 5, 7, 9, 11, 13, 15, 2, 6, 10, 14]
-    pages = {
-        s: remote(outp.at[s], kv.at[core, s], p_send.at[s], p_recv.at[s], page_dev(s)) for s in order
-    }
-    for s in (2, 6, 10, 14, 1, 3, 5, 7, 9, 11, 13, 15, 4, 8, 12):
-        pages[s].start()
-    pagef = {
-        s: remote(kv.at[core, s], kv.at[core, s], pf_send.at[s], pf_recv.at[s], partner) for s in range(16)
-    }
-    pagef[0].start()
+    odd = seq % 2
+    near_seq = {"seq": seq + 1 - 2 * odd}
+
+    def page_copy(s, dev):
+        return remote(outp.at[s], kv.at[core, s], p_send.at[s], p_recv.at[s], dev)
+
+    def far_slots(parity, dzs):
+        return [(2 * k + parity) * 4 + dz for dz in dzs for k in range(2)]
+
+    sent = [
+        page_copy(s, {"group": group_to(s), "seq": seq + 1 - 2 * odd}) for s in far_slots(1 - odd, [2])
+    ]
+    sent += [page_copy(s, {"group": group_to(s)}) for s in far_slots(odd, [1, 3]) + [4, 8, 12]]
+    for copy in sent:
+        copy.start()
+
+    def page_pass(s):
+        return remote(kv.at[core, s], kv.at[core, s], z_send.at[s], z_recv.at[s], near_seq)
+
+    def page_share(s):
+        return remote(kv.at[core, s], kv.at[core, s], pf_send.at[s], pf_recv.at[s], partner)
+
+    page_share(0).start()
 
     loads[5].wait()
     at_pos = lax.broadcasted_iota(jnp.int32, (32, 256), 1) + (length + seq * 256)
@@ -246,10 +259,17 @@
             mask,
         )
 
-    def take(slots):
+    def take(slots, passed=False):
         for s in slots:
-            pages[s].wait_recv()
-            pagef[s].start()
+            page_copy(s, partner).wait_recv()
+            if passed:
+                page_pass(s).start()
+            page_share(s).start()
+
+    def take_passed(slots):
+        for s in slots:
+            page_pass(s).wait_recv()
+            page_share(s).start()
 
     def ready(slots):
         for s in slots:
@@ -263,16 +283,19 @@
     take([4, 8, 12])
     new_ready(0)
     fold(fresh[0, 0], fresh[1, 0], lambda s: jnp.where(causal, s, NEG))
-    c0, c1, c2, c3 = [0, 4, 8, 12], [1, 3, 5, 7], [9, 11, 13, 15], [2, 6, 10, 14]
+    c0 = [0, 4, 8, 12]
+    d1, d2 = far_slots(odd, [1, 3]), far_slots(odd, [2])
+    e1, e2 = far_slots(1 - odd, [1, 3]), far_slots(1 - odd, [2])
     ready(c0)
     fold_pages(c0)
-    take(c1)
-    take(c2)
-    ready(c1)
-    fold_pages(c1)
-    take(c3)
-    ready(c2)
-    fold_pages(c2)
+    take(d1, True)
+    take(d2, True)
+    ready(d1)
+    fold_pages(d1)
+    take_passed(e1)
+    take_passed(e2)
+    ready(e1)
+    fold_pages(e1)
     for step in range(1, 4):
         @pl.when(seq >= step)
         def _():
@@ -280,8 +303,8 @@
                 fresh.at[core, 0], fresh.at[core, step], n_send.at[step], n_recv.at[step], {"seq": (seq + step) % 4}
             ).wait_recv()
             newf[step].start()
-    ready(c3)
-    fold_pages(c3)
+    ready(d2 + e2)
+    fold_pages(d2 + e2)
     for step in range(1, 4):
         @pl.when(seq >= step)
         def _():
@@ -335,10 +358,12 @@
 
     for copy in [*first, own_x, *second, *xf, *s1, *s2, s3]:
         copy.wait_send()
-    for s in range(1, 16):
-        pages[s].wait_send()
-    for s in range(16):
-        pagef[s].wait_send()
+    for copy in sent:
+        copy.wait_send()
+    for s in d1 + d2:
+        page_pass(s).wait_send()
+    for s in c0 + d1 + d2 + e1 + e2:
+        page_share(s).wait_send()
     for d in range(4):
         rs[d].wait_send()
     newf[0].wait_send()
@@ -398,7 +423,7 @@
             pltpu.VMEM((3, 256, 256), BF16),
             pltpu.VMEM((256, 256), BF16),
             dma((5,)), dma((5,)), dma((4,)), dma((4,)),
-            dma((16,)), dma((16,)), dma((16,)), dma((16,)),
+            dma((16,)), dma((16,)), dma((16,)), dma((16,)), dma((16,)), dma((16,)),
             dma((4,)), dma((4,)), dma((4,)), dma((4,)),
             dma((4,)), dma((4,)), dma((5,)), dma((5,)),
         ],

time: 51.6 us -> 51.8 us (level)
  the two profiles are of different devices: /device:TPU:2 before, /device:TPU:96 now
where the time goes in v5:
time: 51.8 us; the launch traced here: 51.6 us
  Pallas kernels  50 us (97%)
  local copies, waits for them, and re-layouts  1.57 us (3%)
    pallas_call x1, Pallas kernels, shards(): pl.pallas_call(layer_kernel, out_shape=jax.ShapeDtypeStruct((256, 256), B...  50 us
    unnamed x1, local copies, waits for them, and re-layouts  1.57 us

profile of v5, /device:TPU:96, one launch (start us, length us, event | category | flops | bytes accessed | tf_op | source)
XLA Modules:
  0.0 51.6 jit_solution(10176233511805292340)
XLA Ops:
  0.0 50.0 %shard_map.91 = bf16[256,256]{1,0:T(8,128)(2,1)} custom-call(s32[16]{0:T(128)} %slots_ref.1, s32[16]{0:T(128)} %lengths_ref.1, s32[16,16]{1,0:T(8,128)} %table_ref.1, f32[32,256]{1,0:T(8,128)} %constant.2.clone.freq_hbm, bf16[256,256]{1,0:T(8,128)(2,1)} %bitcast.7, bf16[2048,256]{1,0:T(8,128)(2,1)} %qw_hbm.1, bf16[64,2048]{1,0:T(8,128)(2,1)} %bitcast.5, ...), custom_call_target="tpu_custom_call" | custom-call | tf_op jit(solution)/shard_map/pallas_call | solution.py:392
  50.1 1.6 %copy.11 = bf16[1,256,256]{2,1,0:T(8,128)(2,1)} copy(bf16[1,256,256]{2,1,0:T(8,128)(2,1)} %bitcast.4) | data formatting | bytes 262144

commit v6 on v4

--- a/solution.py
+++ b/solution.py
@@ -74,19 +74,6 @@
 
     mine_req = slots_ref[group]
     length = lengths_ref[mine_req]
-    loads[0].wait()
-
-    def pick(s, carry):
-        req = slots_ref[group_to(s)]
-        at = 0
-        for w in range(16):
-            off = table_ref[req, w] - group * 16
-            at = at + jnp.where((off & -16) == 0, off, 0)
-        outp[s] = pool_ref[at]
-        return carry
-
-    lax.fori_loop(0, 16, pick, 0)
-    kv[core, 0] = outp[0]
     loads[1].wait()
     pl.semaphore_wait(barrier, 21)
 
@@ -102,6 +89,21 @@
     for copy in first:
         copy.start()
     own_x.start()
+
+    loads[0].wait()
+
+    def pick(s, carry):
+        req = slots_ref[group_to(s)]
+        at = 0
+        for w in range(16):
+            off = table_ref[req, w] - group * 16
+            at = at + jnp.where((off & -16) == 0, off, 0)
+        outp[s] = pool_ref[at]
+        return carry
+
+    lax.fori_loop(0, 16, pick, 0)
+    kv[core, 0] = outp[0]
+
     order = [1, 3, 4, 8, 12, 5, 7, 9, 11, 13, 15, 2, 6, 10, 14]
     pages = {
         s: remote(outp.at[s], kv.at[core, s], p_send.at[s], p_recv.at[s], page_dev(s)) for s in order

time: 51.6 us -> 52.1 us (level)
    pallas_call x1, Pallas kernels: 49.8 us -> 50.3 us  [shards(): pl.pallas_call(layer_kernel, out_shape=jax.ShapeDtypeStruct((256, 256), B...]
where the time goes in v6:
time: 52.1 us; the launch traced here: 51.9 us
  Pallas kernels  50.3 us (97%)
  local copies, waits for them, and re-layouts  1.57 us (3%)
    pallas_call x1, Pallas kernels, shards(): pl.pallas_call(layer_kernel, out_shape=jax.ShapeDtypeStruct((256, 256), B...  50.3 us
    unnamed x1, local copies, waits for them, and re-layouts  1.57 us

profile of v6, /device:TPU:2, one launch (start us, length us, event | category | flops | bytes accessed | tf_op | source)
XLA Modules:
  0.0 51.9 jit_solution(3020888630912251829)
XLA Ops:
  0.0 50.3 %shard_map.91 = bf16[256,256]{1,0:T(8,128)(2,1)} custom-call(s32[16]{0:T(128)} %slots_ref.1, s32[16]{0:T(128)} %lengths_ref.1, s32[16,16]{1,0:T(8,128)} %table_ref.1, f32[32,256]{1,0:T(8,128)} %constant.2.clone.freq_hbm, bf16[256,256]{1,0:T(8,128)(2,1)} %bitcast.7, bf16[2048,256]{1,0:T(8,128)(2,1)} %qw_hbm.1, bf16[64,2048]{1,0:T(8,128)(2,1)} %bitcast.5, ...), custom_call_target="tpu_custom_call" | custom-call | tf_op jit(solution)/shard_map/pallas_call | solution.py:369
  50.4 1.6 %copy.11 = bf16[1,256,256]{2,1,0:T(8,128)(2,1)} copy(bf16[1,256,256]{2,1,0:T(8,128)(2,1)} %bitcast.4) | data formatting | bytes 262144

commit v7 on v4

--- a/solution.py
+++ b/solution.py
@@ -213,6 +213,7 @@
 
     def fold(keys, values, mask):
         kb = keys.T
+        summed = jnp.concatenate([values, jnp.ones((16, values.shape[1]), BF16)], axis=0)
 
         def head_pair(i, carry):
             scores = [jnp.dot(kb, qt[2 * i + k], preferred_element_type=F32) for k in range(2)]
@@ -224,8 +225,9 @@
                 p = jnp.exp(s - new)
                 alpha = jnp.exp(old - new)
                 top[h] = new
-                tot[h] = tot[h] * alpha + jnp.sum(p, axis=0, keepdims=True)
-                acc[h] = acc[h] * alpha + jnp.dot(values, p.astype(BF16), preferred_element_type=F32)
+                mixed = jnp.dot(summed, p.astype(BF16), preferred_element_type=F32)
+                tot[h] = tot[h] * alpha + mixed[HD:HD + 1]
+                acc[h] = acc[h] * alpha + mixed[:HD]
             return carry
 
         lax.fori_loop(0, 2, head_pair, 0)

time: 51.6 us -> 51.4 us (level)
  no operation moved by 1% of the time
where the time goes in v7:
time: 51.4 us; the launch traced here: 51.2 us
  Pallas kernels  49.6 us (96%)
  local copies, waits for them, and re-layouts  1.57 us (3%)
    pallas_call x1, Pallas kernels, shards(): pl.pallas_call(layer_kernel, out_shape=jax.ShapeDtypeStruct((256, 256), B...  49.6 us
    unnamed x1, local copies, waits for them, and re-layouts  1.57 us

profile of v7, /device:TPU:2, one launch (start us, length us, event | category | flops | bytes accessed | tf_op | source)
XLA Modules:
  0.0 51.2 jit_solution(1569650982277905296)
XLA Ops:
  0.0 49.6 %shard_map.91 = bf16[256,256]{1,0:T(8,128)(2,1)} custom-call(s32[16]{0:T(128)} %slots_ref.1, s32[16]{0:T(128)} %lengths_ref.1, s32[16,16]{1,0:T(8,128)} %table_ref.1, f32[32,256]{1,0:T(8,128)} %constant.2.clone.freq_hbm, bf16[256,256]{1,0:T(8,128)(2,1)} %bitcast.7, bf16[2048,256]{1,0:T(8,128)(2,1)} %qw_hbm.1, bf16[64,2048]{1,0:T(8,128)(2,1)} %bitcast.5, ...), custom_call_target="tpu_custom_call" | custom-call | tf_op jit(solution)/shard_map/pallas_call | solution.py:369
  49.7 1.6 %copy.11 = bf16[1,256,256]{2,1,0:T(8,128)(2,1)} copy(bf16[1,256,256]{2,1,0:T(8,128)(2,1)} %bitcast.4) | data formatting | bytes 262144
